TPU v7x, 32 devices: a whole 2x2x4 slice. The times are simulated.
32 devices in a mesh: clip: 2 (over x), ord: 16 (over z, y, core).
Axes of the slice: x: 2, y: 2, z: 4, core: 2. Of those that a mesh axis runs over, the one named last changes fastest.
Arguments:
- reflection: bfloat16 [2, 16384, 8192], P(None, ('clip', 'ord')), parts along dimension 1, may hold values from -0.0625 to 0.0625
- incidence: bfloat16 [2, 8192, 16], replicated, may hold values from -6 to 6
- source_shift: int32 [16, 2], P('ord'), may hold values from -8 to 8
- source_weight: float32 [16], P('ord'), may hold values from 0.1 to 1
- grid_map: int32 [4096], replicated, may hold values from 0 to 4095, each once
- pupil_mask: int32 [64, 64], replicated, may hold values 0 or 1
- pupil_phase: float32 [2, 64, 64], replicated, may hold values from -3.140625 to 3.140625
- tile_order: int32 [16], replicated, may hold values from 0 to 15, each once
Outputs:
- aerial: float32 [2048, 2, 1024], P(('clip', 'ord')), parts along dimension 0
There are 2 independent parts, one for each index of `clip`. A program takes and returns all parts, laid end to end along the dimension named above; an argument that names none is the same for every part. Nothing has to cross between parts.
Inputs may be any that keep to these rules, and one draw needn't show every extreme that they name: `grid_map`: a permutation of the 4096 pupil cells. `tile_order`: a permutation of the 16 tiles.
All inputs are finite; a program needn't handle non-finite values.
Results may differ from a plain program's by a relative error of at most 0.0003.
Values may be sent and summed in bfloat16 or wider, within the bound.
A program may use at most 128 MiB of HBM per device.

v0:
```python
import math
import jax
import jax.numpy as jnp
from jax import lax
from jax.sharding import PartitionSpec as P

PIX = 1024
HIGHEST = lax.Precision.HIGHEST


def phase_table(left_ints, right_ints, period):
    turn_index = jnp.mod(left_ints[:, None] * right_ints[None, :], period).astype(jnp.float32)
    angles = turn_index * (2.0 * math.pi / period)
    return (jnp.cos(angles), jnp.sin(angles))


def band_kernel(points, period, grid_side):
    samples = 2 * grid_side
    difference = jnp.arange(1 - grid_side, grid_side, dtype=jnp.int32)
    fine_cos, fine_sin = phase_table(points, difference, period)
    coarse_cos, coarse_sin = phase_table(jnp.arange(samples, dtype=jnp.int32), difference, samples)
    joined = jnp.einsum("pm,cm->pc", fine_cos, coarse_cos, precision=HIGHEST)
    joined = joined + jnp.einsum("pm,cm->pc", fine_sin, coarse_sin, precision=HIGHEST)
    return joined / samples


def tile_lookup(row_index, tile_order, tile_rows):
    tile_number = row_index // tile_rows
    matches = tile_number[:, None] == jnp.arange(tile_order.shape[0], dtype=jnp.int32)[None, :]
    chosen = jnp.sum(jnp.where(matches, tile_order[None, :], 0), axis=1)
    return chosen * tile_rows + row_index % tile_rows


def pupil_amplitude(grid_cells, source_shift, pupil_mask, pupil_phase):
    grid_side = pupil_mask.shape[0]
    item_count = grid_cells.shape[0]
    margin = grid_side // 8
    cells_float = grid_cells.astype(jnp.float32).reshape(item_count, 2, 2, grid_side, grid_side)
    cell_real = cells_float[:, 0]
    cell_imag = cells_float[:, 1]
    open_pad = jnp.pad(pupil_mask.astype(jnp.float32), margin)
    phase_pad = jnp.pad(pupil_phase, ((0, 0), (margin, margin), (margin, margin)))

    def window(one_shift):
        row_start = margin + one_shift[0]
        col_start = margin + one_shift[1]
        opened = lax.dynamic_slice(open_pad, (row_start, col_start), (grid_side, grid_side))
        phased = lax.dynamic_slice(
            phase_pad, (jnp.zeros((), jnp.int32), row_start, col_start), (2, grid_side, grid_side)
        )
        return (opened, phased)

    opened, phased = jax.vmap(window)(source_shift)
    phase_cos = jnp.cos(phased)[:, :, None]
    phase_sin = jnp.sin(phased)[:, :, None]
    open_scale = opened[:, None, None] * (1.0 / math.sqrt(grid_side * grid_side))
    amp_real = (cell_real[:, None] * phase_cos - cell_imag[:, None] * phase_sin) * open_scale
    amp_imag = (cell_real[:, None] * phase_sin + cell_imag[:, None] * phase_cos) * open_scale
    return (amp_real, amp_imag)


def column_pass(amp_real, amp_imag, period, points):
    grid_side = amp_real.shape[-1]
    frequency = jnp.arange(grid_side, dtype=jnp.int32) - grid_side // 2
    cosine_table, sine_table = phase_table(frequency, points, period)
    rows_real = jnp.transpose(amp_real, (3, 0, 1, 2, 4)).reshape(-1, grid_side)
    rows_imag = jnp.transpose(amp_imag, (3, 0, 1, 2, 4)).reshape(-1, grid_side)
    stacked = jnp.concatenate([rows_real, rows_imag], 1)
    to_real = jnp.concatenate([cosine_table, -sine_table], 0)
    to_imag = jnp.concatenate([sine_table, cosine_table], 0)
    part_real = jnp.dot(stacked, to_real, precision=HIGHEST).reshape(grid_side, -1)
    part_imag = jnp.dot(stacked, to_imag, precision=HIGHEST).reshape(grid_side, -1)
    return jnp.concatenate([part_real, part_imag], 0)


def row_power(columns, row_points, period, weights):
    grid_side = columns.shape[0] // 2
    frequency = jnp.arange(grid_side, dtype=jnp.int32) - grid_side // 2
    cosine_table, sine_table = phase_table(row_points, frequency, period)
    row_lift = jnp.concatenate(
        [
            jnp.concatenate([cosine_table, -sine_table], 1),
            jnp.concatenate([sine_table, cosine_table], 1),
        ],
        0,
    )
    field_rows = jnp.dot(row_lift, columns, precision=HIGHEST)
    block_rows = row_points.shape[0]
    powers = (
        field_rows[:block_rows] * field_rows[:block_rows]
        + field_rows[block_rows:] * field_rows[block_rows:]
    )
    powers = powers.reshape(block_rows, weights.shape[0], 2, 2, -1)
    return jnp.einsum("bsfpx,s->bfx", powers, weights, precision=HIGHEST)


def local(
    reflection,
    incidence,
    source_shift,
    source_weight,
    grid_map,
    pupil_mask,
    pupil_phase,
    tile_order,
):
    devices = lax.axis_size("ord")
    local_rows = reflection.shape[1]
    source_count = source_shift.shape[0]
    grid_side = pupil_mask.shape[0]
    order_count = grid_side * grid_side
    pixels = PIX
    real_part = jnp.dot(reflection[0], incidence[0], preferred_element_type=jnp.float32) - jnp.dot(
        reflection[1], incidence[1], preferred_element_type=jnp.float32
    )
    imag_part = jnp.dot(reflection[0], incidence[1], preferred_element_type=jnp.float32) + jnp.dot(
        reflection[1], incidence[0], preferred_element_type=jnp.float32
    )
    fields = jnp.stack([real_part, imag_part]).astype(jnp.bfloat16)
    by_owner = fields.reshape(2, local_rows, devices, source_count)
    inverse = jnp.argsort(grid_map)
    received = lax.all_to_all(by_owner, "ord", split_axis=2, concat_axis=1, tiled=True)
    item_count = received.shape[3]
    ordered = jnp.take(received.reshape(2, 2, order_count, item_count), inverse, axis=2)
    grid_cells = jnp.transpose(ordered, (3, 0, 1, 2))
    amp_real, amp_imag = pupil_amplitude(grid_cells, source_shift, pupil_mask, pupil_phase)
    weights = source_weight / (source_count * devices)
    tile_rows = pixels // devices
    samples = 2 * grid_side
    sample_points = jnp.arange(samples, dtype=jnp.int32)
    columns = column_pass(amp_real, amp_imag, samples, sample_points)
    local_power = row_power(columns, sample_points, samples, weights)
    summed = lax.psum(local_power, "ord")
    row_index = lax.axis_index("ord") * tile_rows + jnp.arange(tile_rows, dtype=jnp.int32)
    image_rows = tile_lookup(row_index, tile_order, tile_rows)
    kernel_rows = band_kernel(image_rows, pixels, grid_side)
    kernel_cols = band_kernel(jnp.arange(pixels, dtype=jnp.int32), pixels, grid_side)
    partial_value = jnp.dot(kernel_rows, summed.reshape(samples, 2 * samples), precision=HIGHEST)
    partial_value = partial_value.reshape(tile_rows * 2, samples)
    aerial = jnp.einsum("rd,xd->rx", partial_value, kernel_cols, precision=HIGHEST).reshape(
        tile_rows, 2, pixels
    )
    return aerial


def solution(mesh):
    in_specs = (P(None, ("clip", "ord"), None), P(), P("ord", None), P("ord"), P(), P(), P(), P())
    out_specs = P(("clip", "ord"), None, None)
    return jax.shard_map(local, mesh=mesh, in_specs=in_specs, out_specs=out_specs, check_vma=False)
```

profile of v0, /device:TPU:8, one launch (start us, length us, event | category | flops | bytes accessed | tf_op | source)
XLA Modules:
  0.0 186.6 jit_solution(11292437768441231674)
XLA Ops:
  6.5 5.8 %fusion.2 = f32[512,16]{0,1:T(8,128)S(1)} fusion(bf16[2,512,8192]{2,1,0:T(8,128)(2,1)} %param.8, bf16[2,8192,16]{1,2,0:T(8,128)(2,1)} %param.9), kind=kOutput, calls=%fused_computation.3 | convolution fusion | flops 134217728 | bytes 8683520 | tf_op jit(solution)/shard_map/dot_general | solution.py:113
  12.3 6.5 %fusion = f32[512,16]{0,1:T(8,128)S(1)} fusion(bf16[2,512,8192]{2,1,0:T(8,128)(2,1)} %param.8, bf16[2,8192,16]{1,2,0:T(8,128)(2,1)} %param.9), kind=kOutput, calls=%fused_computation.1 | convolution fusion | flops 134217728 | bytes 8683520 | tf_op jit(solution)/shard_map/dot_general | solution.py:116
  18.9 2.3 %fusion.29 = bf16[1,512,16,1]{1,2,3,0:T(8,128)(2,1)S(1)} fusion(f32[512,16]{0,1:T(8,128)S(1)} %fusion.2, bf16[2,512,8192]{2,1,0:T(8,128)(2,1)S(1)} %copy-done.4, bf16[2,8192,16]{1,2,0:T(8,128)(2,1)S(1)} %copy-done.5), kind=kOutput, calls=%fused_computation.25 | convolution fusion | flops 134234112 | bytes 8699904 | tf_op jit(solution)/shard_map/dot_general | solution.py:113
  21.1 2.3 %fusion.32 = bf16[1,512,16,1]{1,2,3,0:T(8,128)(2,1)S(1)} fusion(f32[512,16]{0,1:T(8,128)S(1)} %fusion, bf16[2,512,8192]{2,1,0:T(8,128)(2,1)S(1)} %copy-done.4, bf16[2,8192,16]{1,2,0:T(8,128)(2,1)S(1)} %copy-done.5), kind=kOutput, calls=%fused_computation.26 | convolution fusion | flops 134234112 | bytes 8699904 | tf_op jit(solution)/shard_map/dot_general | solution.py:116
  23.4 0.7 copy.39
  24.1 6.3 %all-to-all-start = ((bf16[2,512,16,1]{1,0,3,2:T(2,128)(2,1)}), bf16[2,512,16,1]{1,0,3,2:T(2,128)(2,1)S(1)}, u32[]{:S(2)}, u32[]{:S(2)}) async-start(bf16[2,512,16,1]{1,0,3,2:T(2,128)(2,1)} %copy.39), calls=%async_computation | async-start | bytes 65536 | tf_op jit(solution)/shard_map/all_to_all | solution.py:122
  30.6 0.6 fusion.151
  33.8 5.8 %sort.17 = (s32[4096]{0:T(1024)}, s32[4096]{0:T(1024)S(1)}) sort(s32[4096]{0:T(1024)S(1)} %copy-done.2, s32[4096]{0:T(1024)S(1)} %iota.72), dimensions={0}, to_apply=%region_1.2 | sort | flops 49152 | bytes 65536 | tf_op jit(solution)/shard_map/jit(argsort)/sort | solution.py:121
  41.6 2.7 %fusion.39 = f32[1024,128]{1,0:T(8,128)S(1)} fusion(s32[127]{0:T(128)S(1)} %iota_add_fusion.1), kind=kOutput, calls=%fused_computation.34 | convolution fusion | flops 201801984 | bytes 524796 | tf_op jit(solution)/shard_map/pm,cm->pc/dot_general | solution.py:22
  44.3 0.6 fusion.103
  44.9 2.7 %fusion.14 = f32[1024,128,1]{1,0,2:T(8,128)S(1)} fusion(f32[1024,128]{1,0:T(8,128)S(1)} %fusion.39, s32[127]{0:T(128)S(1)} %iota_add_fusion.1), kind=kOutput, calls=%fused_computation.17 | convolution fusion | flops 202064128 | bytes 1049084 | tf_op jit(solution)/shard_map/pm,cm->pc/dot_general | solution.py:23
  47.8 4.1 %copy.41 = bf16[2,2,4096]{1,0,2:T(2,128)(2,1)} copy(bf16[2,2,4096]{2,1,0:T(2,128)(2,1)S(1)} %reshape.285) | data formatting | bytes 65536 | tf_op jit(solution)/shard_map/reshape | solution.py:124
  51.9 15.4 %gather_fusion = bf16[4096,2,2]{2,1,0:T(2,128)(2,1)S(1)} fusion(bf16[2,2,4096]{1,0,2:T(2,128)(2,1)} %copy.41, s32[4096]{0:T(1024)S(1)} %fusion.116), kind=kCustom, calls=%fused_computation | custom fusion | bytes 81920 | tf_op jit(solution)/shard_map/jit(_take)/gather | solution.py:124
  67.2 5.8 %fusion.12 = f32[1,2,2,64,64]{2,1,4,3,0:T(2,128)S(1)} fusion(bf16[1,2,2,64,64]{2,1,4,3,0:T(2,128)(2,1)S(1)} %bitcast.80, pred[64,64]{1,0:T(8,128)(4,1)S(1)} %broadcast_in_dim.32), kind=kLoop, calls=%fused_computation.14 | loop fusion | flops 32768 | bytes 102400 | tf_op jit(solution)/shard_map/convert_element_type | solution.py:38
  73.0 6.1 %fusion.150 = (f32[1,1,2,64,64]{2,1,4,3,0:T(1,128)}, f32[1,1,2,64,64]{2,1,4,3,0:T(1,128)S(1)}) fusion(f32[1,2,2,64,64]{2,1,4,3,0:T(2,128)S(1)} %fusion.12), kind=kLoop, calls=%fused_computation.173 | loop fusion | bytes 131072 | tf_op jit(solution)/shard_map/slice | solution.py:39
  79.1 2.3 %copy.42 = f32[2,64,64]{2,0,1:T(2,128)S(1)} copy(f32[2,64,64]{0,2,1:T(8,128)} %bitcast.79) | data formatting | bytes 65536 | tf_op jit(solution)/shard_map/mul | solution.py:57
  81.4 0.7 copy.44
  83.0 0.6 fusion.45
  84.2 0.8 copy.48
  85.0 0.6 fusion.16
  85.6 91.2 %all-reduce.4.cloned.1.call-done = f32[2,128,128]{2,1,0:T(8,128)} async-done(((f32[2,128,128]{2,1,0:T(8,128)}), f32[2,128,128]{2,1,0:T(8,128)}) %all-reduce.4.cloned.1.call-update) | async-done | bytes 131088 | tf_op jit(solution)/shard_map/psum | solution.py:133
  176.8 1.2 fusion.152
  177.9 0.6 fusion.153
  178.5 1.2 copy.47
  (45 shorter events, 3.2 us)
Async XLA Ops:
  6.5 12.3 %copy-start.4 = (bf16[2,512,8192]{2,1,0:T(8,128)(2,1)S(1)}, bf16[2,512,8192]{2,1,0:T(8,128)(2,1)}, u32[]{:S(2)}) copy-start(bf16[2,512,8192]{2,1,0:T(8,128)(2,1)} %param.8) | copy-start | bytes 50331652
  6.5 12.3 %copy-start.5 = (bf16[2,8192,16]{1,2,0:T(8,128)(2,1)S(1)}, bf16[2,8192,16]{1,2,0:T(8,128)(2,1)}, u32[]{:S(2)}) copy-start(bf16[2,8192,16]{1,2,0:T(8,128)(2,1)} %param.9) | copy-start | bytes 1572868
  18.8 11.8 %copy-start.3 = (s32[1,2]{1,0:T(1,128)S(1)}, s32[1,2]{1,0:T(1,128)}, u32[]{:S(2)}) copy-start(s32[1,2]{1,0:T(1,128)} %param.10) | copy-start | bytes 28
  18.8 14.9 %copy-start.2 = (s32[4096]{0:T(1024)S(1)}, s32[4096]{0:T(1024)}, u32[]{:S(2)}) copy-start(s32[4096]{0:T(1024)} %param.12) | copy-start | bytes 49156
  18.8 21.2 %copy-start = (f32[2,64,64]{2,1,0:T(8,128)S(1)}, f32[2,64,64]{2,1,0:T(8,128)}, u32[]{:S(2)}) copy-start(f32[2,64,64]{2,1,0:T(8,128)} %param.14) | copy-start | bytes 98308
  21.1 19.6 %copy-start.1 = (s32[64,64]{1,0:T(8,128)S(1)}, s32[64,64]{1,0:T(8,128)}, u32[]{:S(2)}) copy-start(s32[64,64]{1,0:T(8,128)} %param.13) | copy-start | bytes 49156
  21.1 20.4 %copy-start.6 = (s32[16]{0:T(128)S(1)}, s32[16]{0:T(128)}, u32[]{:S(2)}) copy-start(s32[16]{0:T(128)} %param.15) | copy-start | bytes 196
  24.1 23.6 %all-to-all-start = ((bf16[2,512,16,1]{1,0,3,2:T(2,128)(2,1)}), bf16[2,512,16,1]{1,0,3,2:T(2,128)(2,1)S(1)}, u32[]{:S(2)}, u32[]{:S(2)}) async-start(bf16[2,512,16,1]{1,0,3,2:T(2,128)(2,1)} %copy.39), calls=%async_computation | async-start | bytes 65536 | tf_op jit(solution)/shard_map/all_to_all | solution.py:122
  30.4 146.4 %all-reduce.4.cloned.1.call-start = ((), (), s32[]{:S(2)}) async-start(), calls=%async_computation.1 | async-start | bytes 262144 | tf_op jit(solution)/shard_map/psum | solution.py:133
Sparse Core Ops, SparseCore 0:
  85.1 91.5 all-reduce.3
where the time goes:
time: 187 us
  waiting for transfers between devices  91.2 us (49%)
  local copies, waits for them, and re-layouts  32.8 us (18%)
  matrix products  26.4 us (14%)
  between operations  16.9 us (9%)
  other arithmetic  12.9 us (7%)
  starting transfers between devices  6.51 us (3%)
    psum x1, waiting for transfers between devices, local(): summed = lax.psum(local_power, 'ord')  91.2 us
    gather x1, local copies, waits for them, and re-layouts, local(): jnp.take(received.reshape(2, 2, order_count, item_count), inverse, axis=2)  15.4 us
    dot_general x1, matrix products, local(): jnp.dot(reflection[1], incidence[0], preferred_element_type=jnp.float32)  6.47 us
    all_to_all x1, starting transfers between devices, local(): lax.all_to_all(by_owner, 'ord', split_axis=2, concat_axis=1, tiled=True)  6.3 us
    slice x1, local copies, waits for them, and re-layouts, pupil_amplitude(): cell_real = cells_float[:, 0]  6.12 us
    dot_general x1, matrix products, local(): jnp.dot(reflection[1], incidence[1], preferred_element_type=jnp.float32)  5.79 us
    sort x1, other arithmetic, local(): inverse = jnp.argsort(grid_map)  5.77 us
    convert_element_type x1, other arithmetic, pupil_amplitude(): grid_cells.astype(jnp.float32)  5.76 us
  transfers between devices with their start and end apart: 2, of which 1 were waited for; matrix products, arithmetic and copies ran while one was open for 8% of the time, Pallas kernels for 0%

commit v1 on v0

--- a/solution.py
+++ b/solution.py
@@ -130,7 +130,7 @@
     sample_points = jnp.arange(samples, dtype=jnp.int32)
     columns = column_pass(amp_real, amp_imag, samples, sample_points)
     local_power = row_power(columns, sample_points, samples, weights)
-    summed = lax.psum(local_power, "ord")
+    summed = jnp.sum(lax.all_gather(local_power, "ord"), axis=0)
     row_index = lax.axis_index("ord") * tile_rows + jnp.arange(tile_rows, dtype=jnp.int32)
     image_rows = tile_lookup(row_index, tile_order, tile_rows)
     kernel_rows = band_kernel(image_rows, pixels, grid_side)

time: 187 us -> 134 us (0.72)
  the two profiles are of different devices: /device:TPU:8 before, /device:TPU:0 now
where the time goes in v1:
time: 134 us
  waiting for transfers between devices  36 us (27%)
  local copies, waits for them, and re-layouts  31.9 us (24%)
  matrix products  25.7 us (19%)
  between operations  16.9 us (13%)
  other arithmetic  15.8 us (12%)
  starting transfers between devices  7.64 us (6%)
    all_gather x1, waiting for transfers between devices, local(): summed = jnp.sum(lax.all_gather(local_power, 'ord'), axis=0)  36 us
    gather x1, local copies, waits for them, and re-layouts, local(): jnp.take(received.reshape(2, 2, order_count, item_count), inverse, axis=2)  15.4 us
    all_to_all x1, starting transfers between devices, local(): lax.all_to_all(by_owner, 'ord', split_axis=2, concat_axis=1, tiled=True)  7.41 us
    dot_general x1, matrix products, local(): jnp.dot(reflection[1], incidence[0], preferred_element_type=jnp.float32)  6.47 us
    slice x1, local copies, waits for them, and re-layouts, pupil_amplitude(): cell_real = cells_float[:, 0]  6.12 us
    dot_general x1, matrix products, local(): jnp.dot(reflection[1], incidence[1], preferred_element_type=jnp.float32)  5.79 us
    sort x1, other arithmetic, local(): inverse = jnp.argsort(grid_map)  5.77 us
    convert_element_type x1, other arithmetic, pupil_amplitude(): grid_cells.astype(jnp.float32)  5.76 us
  transfers between devices with their start and end apart: 2, of which 1 were waited for; matrix products, arithmetic and copies ran while one was open for 11% of the time, Pallas kernels for 0%

profile of v1, /device:TPU:0, one launch (start us, length us, event | category | flops | bytes accessed | tf_op | source)
XLA Modules:
  0.0 133.9 jit_solution(8457137689845953082)
XLA Ops:
  6.5 5.8 %fusion.2 = f32[512,16]{0,1:T(8,128)S(1)} fusion(bf16[2,512,8192]{2,1,0:T(8,128)(2,1)} %param.8, bf16[2,8192,16]{1,2,0:T(8,128)(2,1)} %param.9), kind=kOutput, calls=%fused_computation.3 | convolution fusion | flops 134217728 | bytes 8683520 | tf_op jit(solution)/shard_map/dot_general | solution.py:113
  12.3 6.5 %fusion = f32[512,16]{0,1:T(8,128)S(1)} fusion(bf16[2,512,8192]{2,1,0:T(8,128)(2,1)} %param.8, bf16[2,8192,16]{1,2,0:T(8,128)(2,1)} %param.9), kind=kOutput, calls=%fused_computation.1 | convolution fusion | flops 134217728 | bytes 8683520 | tf_op jit(solution)/shard_map/dot_general | solution.py:116
  18.9 2.3 %fusion.29 = bf16[1,512,16,1]{1,2,3,0:T(8,128)(2,1)S(1)} fusion(f32[512,16]{0,1:T(8,128)S(1)} %fusion.2, bf16[2,512,8192]{2,1,0:T(8,128)(2,1)S(1)} %copy-done.4, bf16[2,8192,16]{1,2,0:T(8,128)(2,1)S(1)} %copy-done.5), kind=kOutput, calls=%fused_computation.25 | convolution fusion | flops 134234112 | bytes 8699904 | tf_op jit(solution)/shard_map/dot_general | solution.py:113
  21.1 2.3 %fusion.32 = bf16[1,512,16,1]{1,2,3,0:T(8,128)(2,1)S(1)} fusion(f32[512,16]{0,1:T(8,128)S(1)} %fusion, bf16[2,512,8192]{2,1,0:T(8,128)(2,1)S(1)} %copy-done.4, bf16[2,8192,16]{1,2,0:T(8,128)(2,1)S(1)} %copy-done.5), kind=kOutput, calls=%fused_computation.26 | convolution fusion | flops 134234112 | bytes 8699904 | tf_op jit(solution)/shard_map/dot_general | solution.py:116
  23.4 0.7 copy.39
  24.1 7.4 %all-to-all-start = ((bf16[2,512,16,1]{1,0,3,2:T(2,128)(2,1)}), bf16[2,512,16,1]{1,0,3,2:T(2,128)(2,1)S(1)}, u32[]{:S(2)}, u32[]{:S(2)}) async-start(bf16[2,512,16,1]{1,0,3,2:T(2,128)(2,1)} %copy.39), calls=%async_computation | async-start | bytes 65536 | tf_op jit(solution)/shard_map/all_to_all | solution.py:122
  31.7 0.6 fusion.151
  34.9 5.8 %sort.17 = (s32[4096]{0:T(1024)}, s32[4096]{0:T(1024)S(1)}) sort(s32[4096]{0:T(1024)S(1)} %copy-done.2, s32[4096]{0:T(1024)S(1)} %iota.72), dimensions={0}, to_apply=%region_1.2 | sort | flops 49152 | bytes 65536 | tf_op jit(solution)/shard_map/jit(argsort)/sort | solution.py:121
  42.7 3.9 %copy.41 = bf16[2,2,4096]{1,0,2:T(2,128)(2,1)} copy(bf16[2,2,4096]{2,1,0:T(2,128)(2,1)S(1)} %reshape.285) | data formatting | bytes 65536 | tf_op jit(solution)/shard_map/reshape | solution.py:124
  46.6 15.4 %gather_fusion = bf16[4096,2,2]{2,1,0:T(2,128)(2,1)S(1)} fusion(bf16[2,2,4096]{1,0,2:T(2,128)(2,1)} %copy.41, s32[4096]{0:T(1024)S(1)} %fusion.116), kind=kCustom, calls=%fused_computation | custom fusion | bytes 81920 | tf_op jit(solution)/shard_map/jit(_take)/gather | solution.py:124
  62.0 5.8 %fusion.12 = f32[1,2,2,64,64]{2,1,4,3,0:T(2,128)S(1)} fusion(bf16[1,2,2,64,64]{2,1,4,3,0:T(2,128)(2,1)S(1)} %bitcast.84, pred[64,64]{1,0:T(8,128)(4,1)S(1)} %broadcast_in_dim.32), kind=kLoop, calls=%fused_computation.14 | loop fusion | flops 32768 | bytes 102400 | tf_op jit(solution)/shard_map/convert_element_type | solution.py:38
  67.8 6.1 %fusion.150 = (f32[1,1,2,64,64]{2,1,4,3,0:T(1,128)}, f32[1,1,2,64,64]{2,1,4,3,0:T(1,128)S(1)}) fusion(f32[1,2,2,64,64]{2,1,4,3,0:T(2,128)S(1)} %fusion.12), kind=kLoop, calls=%fused_computation.174 | loop fusion | bytes 131072 | tf_op jit(solution)/shard_map/slice | solution.py:39
  73.9 2.3 %copy.42 = f32[2,64,64]{2,0,1:T(2,128)S(1)} copy(f32[2,64,64]{0,2,1:T(8,128)} %bitcast.83) | data formatting | bytes 65536 | tf_op jit(solution)/shard_map/mul | solution.py:57
  76.2 0.7 copy.44
  77.8 0.6 fusion.45
  79.0 0.7 broadcast_multiply_fusion
  79.8 0.6 fusion.103
  80.4 0.6 fusion.16
  81.0 2.7 %fusion.39 = f32[1024,128]{1,0:T(8,128)S(1)} fusion(s32[127]{0:T(128)S(1)} %iota_add_fusion.1), kind=kOutput, calls=%fused_computation.34 | convolution fusion | flops 201801984 | bytes 524796 | tf_op jit(solution)/shard_map/pm,cm->pc/dot_general | solution.py:22
  83.7 2.9 %fusion.14 = f32[1024,128,1]{1,0,2:T(8,128)S(1)} fusion(f32[1024,128]{1,0:T(8,128)S(1)} %fusion.39, s32[127]{0:T(128)S(1)} %iota_add_fusion.1), kind=kOutput, calls=%fused_computation.17 | convolution fusion | flops 202064128 | bytes 1049084 | tf_op jit(solution)/shard_map/pm,cm->pc/dot_general | solution.py:23
  86.6 36.0 %all-gather.3.cloned.1.call-done = f32[2048,2,128]{2,1,0:T(2,128)} async-done(((f32[128,2,128]{2,1,0:T(2,128)}), f32[2048,2,128]{2,1,0:T(2,128)}) %all-gather.3.cloned.1.call-update) | async-done | bytes 2097168 | tf_op jit(solution)/shard_map/all_gather | solution.py:133
  122.6 2.3 %reduce_sum.29 = f32[128,2,128]{2,1,0:T(2,128)S(1)} reduce(f32[16,128,2,128]{3,2,1,0:T(2,128)} %bitcast.85, f32[]{:T(128)} %constant.136.clone.1), dimensions={0}, to_apply=%region_3.4 | reduce | flops 491520 | bytes 2228228 | tf_op jit(solution)/shard_map/reduce_sum | solution.py:133
  125.3 0.6 fusion.153
  125.9 1.2 copy.47
  (47 shorter events, 3.6 us)
Async XLA Ops:
  6.5 12.3 %copy-start.4 = (bf16[2,512,8192]{2,1,0:T(8,128)(2,1)S(1)}, bf16[2,512,8192]{2,1,0:T(8,128)(2,1)}, u32[]{:S(2)}) copy-start(bf16[2,512,8192]{2,1,0:T(8,128)(2,1)} %param.8) | copy-start | bytes 50331652
  6.5 12.3 %copy-start.5 = (bf16[2,8192,16]{1,2,0:T(8,128)(2,1)S(1)}, bf16[2,8192,16]{1,2,0:T(8,128)(2,1)}, u32[]{:S(2)}) copy-start(bf16[2,8192,16]{1,2,0:T(8,128)(2,1)} %param.9) | copy-start | bytes 1572868
  18.8 12.9 %copy-start.3 = (s32[1,2]{1,0:T(1,128)S(1)}, s32[1,2]{1,0:T(1,128)}, u32[]{:S(2)}) copy-start(s32[1,2]{1,0:T(1,128)} %param.10) | copy-start | bytes 28
  18.8 16.0 %copy-start.2 = (s32[4096]{0:T(1024)S(1)}, s32[4096]{0:T(1024)}, u32[]{:S(2)}) copy-start(s32[4096]{0:T(1024)} %param.12) | copy-start | bytes 49156
  18.8 22.4 %copy-start = (f32[2,64,64]{2,1,0:T(8,128)S(1)}, f32[2,64,64]{2,1,0:T(8,128)}, u32[]{:S(2)}) copy-start(f32[2,64,64]{2,1,0:T(8,128)} %param.14) | copy-start | bytes 98308
  21.1 20.7 %copy-start.1 = (s32[64,64]{1,0:T(8,128)S(1)}, s32[64,64]{1,0:T(8,128)}, u32[]{:S(2)}) copy-start(s32[64,64]{1,0:T(8,128)} %param.13) | copy-start | bytes 49156
  24.1 18.6 %all-to-all-start = ((bf16[2,512,16,1]{1,0,3,2:T(2,128)(2,1)}), bf16[2,512,16,1]{1,0,3,2:T(2,128)(2,1)S(1)}, u32[]{:S(2)}, u32[]{:S(2)}) async-start(bf16[2,512,16,1]{1,0,3,2:T(2,128)(2,1)} %copy.39), calls=%async_computation | async-start | bytes 65536 | tf_op jit(solution)/shard_map/all_to_all | solution.py:122
  31.5 91.1 %all-gather.3.cloned.1.call-start = ((), (), s32[]{:S(2)}) async-start(), calls=%async_computation.1 | async-start | bytes 2228224 | tf_op jit(solution)/shard_map/all_gather | solution.py:133
  67.8 12.0 %copy-start.6 = (s32[16]{0:T(128)S(1)}, s32[16]{0:T(128)}, u32[]{:S(2)}) copy-start(s32[16]{0:T(128)} %param.15) | copy-start | bytes 196
Sparse Core Ops, SparseCore 0:
  79.8 42.7 all-gather.2
